TPU v7x, 128 devices: a whole 4x4x4 slice. The times are simulated.
128 devices in a mesh: row: 8 (over y, core), col: 16 (over x, z).
Axes of the slice: x: 4, y: 4, z: 4, core: 2. Of those that a mesh axis runs over, the one named last changes fastest.
Arguments:
- tensor_tiles: bfloat16 [512, 128, 128, 128], P(('row', 'col')), may hold values from -384 to 384
- tile_mode1: int32 [512], P(('row', 'col')), may hold values from 0 to 1023, as said below
- tile_mode2: int32 [512], P(('row', 'col')), may hold values from 0 to 127
- tile_mode3: int32 [512], P(('row', 'col')), may hold values from 0 to 63
- factor_mode2: bfloat16 [48, 16384], P(None, 'col'), may hold values from -1 to 1
- factor_mode3: bfloat16 [48, 8192], P(None, 'row'), may hold values from -1 to 1
Outputs:
- factor_mode1: float32 [48, 131072], P(None, ('row', 'col'))
Inputs may be any that keep to these rules, and one draw needn't show every extreme that they name: `tile_mode1`: tiles at positions g*64 to (g+1)*64 - 1 have mode-1 blocks in g*128 to (g+1)*128 - 1; the 4 tiles at positions d*4 to (d+1)*4 - 1 have mode-1 blocks in distinct groups of 8 consecutive blocks (block // 8 all different).
All inputs are finite; a program needn't handle non-finite values.
Results may differ from a plain program's by a relative error of at most 0.0003.
Values may be sent and summed in bfloat16 or wider, within the bound.
No kernel may reach another device: no remote copies, remote signals or barrier semaphores. Data moves between devices by JAX's collectives and lax.ppermute only.
A program may use at most 128 MiB of HBM per device.

v0:
```python
import jax
import jax.numpy as jnp
from jax import lax
from jax.sharding import PartitionSpec as P

IB_DEV = 8
ridge_term = 0.5


def body(tensor_tiles, tile_mode1, tile_mode2, tile_mode3, factor_mode2, factor_mode3):
    rank_count = factor_mode2.shape[0]
    tile_edge = tensor_tiles.shape[1]
    gram_two = lax.psum(
        jnp.dot(factor_mode2, factor_mode2.T, preferred_element_type=jnp.float32), "col"
    )
    gram_three = lax.psum(
        jnp.dot(factor_mode3, factor_mode3.T, preferred_element_type=jnp.float32), "row"
    )
    system = gram_two * gram_three + ridge_term * jnp.eye(rank_count, dtype=jnp.float32)
    full_two = lax.all_gather(factor_mode2, "col", axis=1, tiled=True)
    full_three = lax.all_gather(factor_mode3, "row", axis=1, tiled=True)
    mode2_rows = jnp.transpose(
        full_two.reshape(rank_count, -1, tile_edge)[:, tile_mode2], (1, 0, 2)
    )
    mode3_rows = jnp.transpose(
        full_three.reshape(rank_count, -1, tile_edge)[:, tile_mode3], (1, 0, 2)
    )
    contracted = jnp.einsum(
        "trc,tabc->trab", mode3_rows, tensor_tiles, preferred_element_type=jnp.float32
    )
    tile_rows = jnp.einsum(
        "trab,trb->tra", contracted, mode2_rows.astype(jnp.float32), precision=lax.Precision.HIGHEST
    )
    col_count = lax.axis_size("col")
    row_blocks = IB_DEV * col_count
    local_blocks = tile_mode1 - lax.axis_index("row") * row_blocks
    selector = (local_blocks[:, None] == jnp.arange(row_blocks, dtype=jnp.int32)[None, :]).astype(
        jnp.float32
    )
    row_partials = jnp.einsum("tra,tb->rba", tile_rows, selector, precision=lax.Precision.HIGHEST)
    row_partials = row_partials.reshape(rank_count, row_blocks * tile_edge)
    right_side = lax.psum_scatter(row_partials, "col", scatter_dimension=1, tiled=True)
    cholesky_factor = jnp.linalg.cholesky(system)
    middle = lax.linalg.triangular_solve(cholesky_factor, right_side, left_side=True, lower=True)
    return lax.linalg.triangular_solve(
        cholesky_factor, middle, left_side=True, lower=True, transpose_a=True
    )


def solution(mesh):
    in_specs = (
        P(("row", "col"), None, None, None),
        P(("row", "col")),
        P(("row", "col")),
        P(("row", "col")),
        P(None, "col"),
        P(None, "row"),
    )
    out_specs = P(None, ("row", "col"))
    return jax.shard_map(body, mesh=mesh, in_specs=in_specs, out_specs=out_specs, check_vma=False)
```

profile of v0, /device:TPU:0, one launch (start us, length us, event | category | flops | bytes accessed | tf_op | source)
XLA Modules:
  0.0 194.9 jit_solution(6708601685298031785)
XLA Ops:
  6.5 0.0 all-gather.2.cloned.1.call-start
  6.5 0.7 all-gather.2.cloned.1.call-update
  7.3 0.0 reduce-scatter.2.cloned.1.call-start
  7.3 0.7 compare_select_fusion.1
  8.0 14.2 %all_gather.6 = bf16[48,8192]{1,0:T(8,128)(2,1)S(1)} all-gather(bf16[48,1024]{1,0:T(8,128)(2,1)} %param.11), channel_id=1, replica_groups=mesh['row'=8,'col'=16] {'row'}, dimensions={1}, use_global_device_ids=true | all-gather | bytes 884736 | tf_op jit(solution)/shard_map/all_gather | solution.py:21
  22.2 0.1 copy_bitcast_fusion.2
  22.3 0.6 gather_fusion
  22.9 0.7 compare_select_fusion
  23.6 0.7 broadcast_subtract_fusion
  24.2 12.1 %fusion.6 = f32[4,48,128,128]{3,1,2,0:T(8,128)} fusion(bf16[4,128,128,128]{3,2,1,0:T(8,128)(2,1)} %param.6, bf16[4,48,128]{2,1,0:T(8,128)(2,1)S(1)} %gather_fusion), kind=kOutput, calls=%fused_computation.11 | convolution fusion | flops 805306368 | bytes 29409280 | tf_op jit(solution)/shard_map/trc,tabc->trab/dot_general | solution.py:28
  36.3 19.6 %all-gather.2.cloned.1.call-done = bf16[48,16384]{1,0:T(8,128)(2,1)} async-done(((bf16[48,1024]{1,0:T(8,128)(2,1)}), bf16[48,16384]{1,0:T(8,128)(2,1)}) %all-gather.2.cloned.1.call-update) | async-done | bytes 1572880 | tf_op jit(solution)/shard_map/all_gather | solution.py:20
  55.9 1.7 copy_bitcast_fusion.1
  57.6 0.6 gather_fusion.1
  58.1 0.0 copy-start.1
  58.1 0.0 copy-start
  58.2 16.7 %fusion = f32[4,48,1,128]{3,2,1,0:T(1,128)S(1)} fusion(f32[4,48,128,128]{3,1,2,0:T(8,128)} %fusion.6, bf16[4,48,128,1]{2,1,0,3:T(8,128)(2,1)S(1)} %bitcast.47), kind=kOutput, calls=%fused_computation.2 | convolution fusion | flops 37748736 | bytes 12730368 | tf_op jit(solution)/shard_map/trab,trb->tra/dot_general | solution.py:31
  74.9 1.5 fusion.2
  76.4 3.5 %copy.30 = f32[6,8,128,128]{3,1,2,0:T(8,128)} copy(f32[6,8,128,128]{3,2,1,0:T(8,128)S(1)} %bitcast.46) | data formatting | bytes 6291456
  79.8 0.0 reduce-scatter.2.cloned.1.call-update
  79.9 0.0 copy-done.1
  79.9 0.1 fusion.17
  80.0 72.5 %psum.14 = f32[48,48]{1,0:T(8,128)S(1)} all-reduce(f32[48,48]{1,0:T(8,128)S(1)} %fusion.17), channel_id=1, replica_groups=mesh['row'=8,'col'=16] {'col'}, use_global_device_ids=true, to_apply=%region_0.0 | all-reduce | flops 2304 | bytes 18432 | tf_op jit(solution)/shard_map/psum | solution.py:13
  152.5 0.0 copy-done
  152.5 0.1 fusion.18
  152.7 23.6 %psum.15 = f32[48,48]{1,0:T(8,128)S(1)} all-reduce(f32[48,48]{1,0:T(8,128)S(1)} %fusion.18), channel_id=1, replica_groups=mesh['row'=8,'col'=16] {'row'}, use_global_device_ids=true, to_apply=%region_1.0 | all-reduce | flops 2304 | bytes 18432 | tf_op jit(solution)/shard_map/psum | solution.py:16
  176.3 0.1 copy.9
  176.4 4.4 %cholesky.16 = f32[48,48]{1,0:T(8,128)S(1)} custom-call(f32[48,48]{1,0:T(8,128)S(1)} %fusion.13), custom_call_target="Cholesky" | custom-call | tf_op jit(solution)/shard_map/jit(cholesky)/cholesky | solution.py:43
  180.8 0.6 compare_reduce_fusion
  181.4 0.7 fusion.8
  182.1 3.7 %custom-call.8 = f32[1,48,48]{1,2,0:T(8,128)S(1)} custom-call(f32[1,48,48]{2,1,0:T(8,128)S(1)} %fusion.8), custom_call_target="InvertDiagBlocksLowerTriangular" | custom-call | tf_op jit(solution)/shard_map/triangular_solve | solution.py:45
  185.8 0.0 reduce-scatter.2.cloned.1.call-done
  185.8 1.3 fusion.11
  187.1 1.0 fusion.9
  (5 shorter events, 0.1 us)
Async XLA Ops:
  6.5 49.4 %all-gather.2.cloned.1.call-start = ((), (), s32[]{:S(2)}) async-start(), calls=%async_computation.1 | async-start | bytes 1671168 | tf_op jit(solution)/shard_map/all_gather | solution.py:20
  7.3 178.5 %reduce-scatter.2.cloned.1.call-start = ((), (), s32[]{:S(2)}) async-start(), calls=%async_computation.2 | async-start | bytes 3342336 | tf_op jit(solution)/shard_map/reduce_scatter | solution.py:42
  58.1 21.7 %copy-start.1 = (bf16[48,1024]{1,0:T(8,128)(2,1)S(1)}, bf16[48,1024]{1,0:T(8,128)(2,1)}, u32[]{:S(2)}) copy-start(bf16[48,1024]{1,0:T(8,128)(2,1)} %param.10) | copy-start | bytes 294916
  58.1 94.4 %copy-start = (bf16[48,1024]{1,0:T(8,128)(2,1)S(1)}, bf16[48,1024]{1,0:T(8,128)(2,1)}, u32[]{:S(2)}) copy-start(bf16[48,1024]{1,0:T(8,128)(2,1)} %param.11) | copy-start | bytes 294916
Sparse Core Ops, SparseCore 0:
  9.5 46.3 all-gather.1
  80.0 76.1 reduce-scatter.1
where the time goes:
time: 195 us
  blocking collectives  110 us (56%)
  matrix products  32.8 us (17%)
  waiting for transfers between devices  20.3 us (10%)
  between operations  13.5 us (7%)
  other arithmetic  11.4 us (6%)
  local copies, waits for them, and re-layouts  6.49 us (3%)
    psum x1, blocking collectives, body(): lax.psum(jnp.dot(factor_mode2, factor_mode2.T, preferred_element_type=jnp...  72.5 us
    psum x1, blocking collectives, body(): lax.psum(jnp.dot(factor_mode3, factor_mode3.T, preferred_element_type=jnp...  23.6 us
    all_gather x1, waiting for transfers between devices, body(): full_two = lax.all_gather(factor_mode2, 'col', axis=1, tiled=True)  19.6 us
    dot_general x1, matrix products, body(): jnp.einsum('trab,trb->tra', contracted, mode2_rows.astype(jnp.float32), p...  16.7 us
    all_gather x1, blocking collectives, body(): full_three = lax.all_gather(factor_mode3, 'row', axis=1, tiled=True)  14.2 us
    dot_general x1, matrix products, body(): jnp.einsum('trc,tabc->trab', mode3_rows, tensor_tiles, preferred_element_...  12.1 us
    another operation x3, other arithmetic, body(): cholesky_factor = jnp.linalg.cholesky(system)  5.05 us
    another operation x2, other arithmetic, body(): lax.linalg.triangular_solve(cholesky_factor, middle, left_side=True, lowe...  4.32 us
  transfers between devices with their start and end apart: 2, of which 1 were waited for; matrix products, arithmetic and copies ran while one was open for 13% of the time, Pallas kernels for 0%

commit v1 on v0

--- a/solution.py
+++ b/solution.py
@@ -5,6 +5,11 @@
 
 IB_DEV = 8
 ridge_term = 0.5
+
+
+def swapped_in(shard, axis, dim):
+    repeated = jnp.stack([shard] * lax.axis_size(axis))
+    return jnp.concatenate(lax.all_to_all(repeated, axis, 0, 0), axis=dim)
 
 
 def body(tensor_tiles, tile_mode1, tile_mode2, tile_mode3, factor_mode2, factor_mode3):
@@ -17,7 +22,7 @@
         jnp.dot(factor_mode3, factor_mode3.T, preferred_element_type=jnp.float32), "row"
     )
     system = gram_two * gram_three + ridge_term * jnp.eye(rank_count, dtype=jnp.float32)
-    full_two = lax.all_gather(factor_mode2, "col", axis=1, tiled=True)
+    full_two = swapped_in(factor_mode2, "col", 1)
     full_three = lax.all_gather(factor_mode3, "row", axis=1, tiled=True)
     mode2_rows = jnp.transpose(
         full_two.reshape(rank_count, -1, tile_edge)[:, tile_mode2], (1, 0, 2)

time: 195 us -> 188 us (0.964)
  waiting for transfers between devices: 20.3 us -> 0.02 us
  starting transfers between devices: 0.04 us -> 8.03 us
  local copies, waits for them, and re-layouts: 6.49 us -> 9.7 us
  blocking collectives: 110 us -> 113 us
    all_gather x1 -> x0, waiting for transfers between devices: 19.6 us -> none  [body(): full_two = lax.all_gather(factor_mode2, 'col', axis=1, tiled=True)]
    all_to_all x0 -> x1, starting transfers between devices: none -> 7.99 us  [swapped_in(): return jnp.concatenate(lax.all_to_all(repeated, axis, 0, 0), axis=dim)]
    another operation x0 -> x3, local copies, waits for them, and re-layouts: none -> 4.03 us  [the longest x1 2.28 us: swapped_in(): repeated = jnp.stack([shard] * lax.axis_size(axis))]
    psum x1, blocking collectives: 72.5 us -> 74.9 us  [body(): lax.psum(jnp.dot(factor_mode2, factor_mode2.T, preferred_element_type=jnp...]
  transfers between devices with their start and end apart: 2 -> 2, of which waited for: 1 -> 0; matrix products, arithmetic and copies ran while one was open for 13% -> 13% of each run, Pallas kernels for 0% -> 0%
where the time goes in v1:
time: 188 us
  blocking collectives  113 us (60%)
  matrix products  32.8 us (17%)
  between operations  13.6 us (7%)
  other arithmetic  11.4 us (6%)
  local copies, waits for them, and re-layouts  9.7 us (5%)
  starting transfers between devices  8.03 us (4%)
    psum x1, blocking collectives, body(): lax.psum(jnp.dot(factor_mode2, factor_mode2.T, preferred_element_type=jnp...  74.9 us
    psum x1, blocking collectives, body(): lax.psum(jnp.dot(factor_mode3, factor_mode3.T, preferred_element_type=jnp...  23.6 us
    dot_general x1, matrix products, body(): jnp.einsum('trab,trb->tra', contracted, mode2_rows.astype(jnp.float32), p...  16.7 us
    all_gather x1, blocking collectives, body(): full_three = lax.all_gather(factor_mode3, 'row', axis=1, tiled=True)  14.1 us
    dot_general x1, matrix products, body(): jnp.einsum('trc,tabc->trab', mode3_rows, tensor_tiles, preferred_element_...  12.1 us
    all_to_all x1, starting transfers between devices, swapped_in(): return jnp.concatenate(lax.all_to_all(repeated, axis, 0, 0), axis=dim)  7.99 us
    another operation x3, other arithmetic, body(): cholesky_factor = jnp.linalg.cholesky(system)  5.05 us
    another operation x2, other arithmetic, body(): lax.linalg.triangular_solve(cholesky_factor, middle, left_side=True, lowe...  4.32 us
  transfers between devices with their start and end apart: 2, of which 0 were waited for; matrix products, arithmetic and copies ran while one was open for 13% of the time, Pallas kernels for 0%

profile of v1, /device:TPU:0, one launch (start us, length us, event | category | flops | bytes accessed | tf_op | source)
XLA Modules:
  0.0 188.1 jit_solution(14125661927677147584)
XLA Ops:
  6.5 2.3 %stack.2 = bf16[16,48,1024]{2,1,0:T(8,128)(2,1)} broadcast(bf16[48,1024]{1,0:T(8,128)(2,1)} %param.10), dimensions={1,2} | broadcast | bytes 1671168 | tf_op jit(solution)/shard_map/stack | solution.py:11
  8.8 8.0 %all-to-all-start = ((bf16[16,48,1024]{2,1,0:T(8,128)(2,1)}), bf16[16,48,1024]{2,1,0:T(8,128)(2,1)S(1)}, u32[]{:S(2)}, u32[]{:S(2)}) async-start(bf16[16,48,1024]{2,1,0:T(8,128)(2,1)} %stack.2), calls=%async_computation | async-start | bytes 3145728 | tf_op jit(solution)/shard_map/all_to_all | solution.py:12
  16.8 0.0 reduce-scatter.2.cloned.1.call-start
  16.9 0.7 compare_select_fusion
  17.5 0.7 compare_select_fusion.1
  18.2 14.1 %all_gather.3 = bf16[48,8192]{1,0:T(8,128)(2,1)S(1)} all-gather(bf16[48,1024]{1,0:T(8,128)(2,1)} %param.11), channel_id=1, replica_groups=mesh['row'=8,'col'=16] {'row'}, dimensions={1}, use_global_device_ids=true | all-gather | bytes 884736 | tf_op jit(solution)/shard_map/all_gather | solution.py:26
  32.3 0.1 copy_bitcast_fusion.1
  32.4 0.6 gather_fusion
  33.0 0.7 broadcast_subtract_fusion
  33.7 12.1 %fusion.6 = f32[4,48,128,128]{3,1,2,0:T(8,128)} fusion(bf16[4,128,128,128]{3,2,1,0:T(8,128)(2,1)} %param.6, bf16[4,48,128]{2,1,0:T(8,128)(2,1)S(1)} %gather_fusion), kind=kOutput, calls=%fused_computation.10 | convolution fusion | flops 805306368 | bytes 29409280 | tf_op jit(solution)/shard_map/trc,tabc->trab/dot_general | solution.py:33
  45.8 0.0 all-to-all-done
  45.8 0.9 copy.15
  46.6 0.7 reshape_reshape.3
  47.4 1.0 copy.16
  48.4 0.6 gather_fusion.1
  49.0 0.0 copy-start
  49.0 0.0 copy-start.1
  49.0 16.7 %fusion = f32[4,48,1,128]{3,2,1,0:T(1,128)S(1)} fusion(f32[4,48,128,128]{3,1,2,0:T(8,128)} %fusion.6, bf16[4,48,128,1]{2,1,0,3:T(8,128)(2,1)S(1)} %bitcast.44), kind=kOutput, calls=%fused_computation.2 | convolution fusion | flops 37748736 | bytes 12730368 | tf_op jit(solution)/shard_map/trab,trb->tra/dot_general | solution.py:36
  65.7 1.5 fusion.2
  67.2 3.5 %copy.33 = f32[6,8,128,128]{3,1,2,0:T(8,128)} copy(f32[6,8,128,128]{3,2,1,0:T(8,128)S(1)} %bitcast.42) | data formatting | bytes 6291456
  70.7 0.0 reduce-scatter.2.cloned.1.call-update
  70.7 0.0 copy-done
  70.7 0.1 fusion.17
  70.9 74.9 %psum.14 = f32[48,48]{1,0:T(8,128)S(1)} all-reduce(f32[48,48]{1,0:T(8,128)S(1)} %fusion.17), channel_id=1, replica_groups=mesh['row'=8,'col'=16] {'col'}, use_global_device_ids=true, to_apply=%region_0.0 | all-reduce | flops 2304 | bytes 18432 | tf_op jit(solution)/shard_map/psum | solution.py:18
  145.7 0.0 copy-done.1
  145.7 0.1 fusion.18
  145.9 23.6 %psum.15 = f32[48,48]{1,0:T(8,128)S(1)} all-reduce(f32[48,48]{1,0:T(8,128)S(1)} %fusion.18), channel_id=1, replica_groups=mesh['row'=8,'col'=16] {'row'}, use_global_device_ids=true, to_apply=%region_1.0 | all-reduce | flops 2304 | bytes 18432 | tf_op jit(solution)/shard_map/psum | solution.py:21
  169.5 0.1 copy.13
  169.6 4.4 %cholesky.16 = f32[48,48]{1,0:T(8,128)S(1)} custom-call(f32[48,48]{1,0:T(8,128)S(1)} %fusion.13), custom_call_target="Cholesky" | custom-call | tf_op jit(solution)/shard_map/jit(cholesky)/cholesky | solution.py:48
  174.0 0.6 compare_reduce_fusion
  174.6 0.7 fusion.8
  175.3 3.7 %custom-call.8 = f32[1,48,48]{1,2,0:T(8,128)S(1)} custom-call(f32[1,48,48]{2,1,0:T(8,128)S(1)} %fusion.8), custom_call_target="InvertDiagBlocksLowerTriangular" | custom-call | tf_op jit(solution)/shard_map/triangular_solve | solution.py:50
  179.0 0.0 reduce-scatter.2.cloned.1.call-done
  179.0 1.3 fusion.11
  180.3 1.0 fusion.9
  (5 shorter events, 0.1 us)
Async XLA Ops:
  8.8 36.9 %all-to-all-start = ((bf16[16,48,1024]{2,1,0:T(8,128)(2,1)}), bf16[16,48,1024]{2,1,0:T(8,128)(2,1)S(1)}, u32[]{:S(2)}, u32[]{:S(2)}) async-start(bf16[16,48,1024]{2,1,0:T(8,128)(2,1)} %stack.2), calls=%async_computation | async-start | bytes 3145728 | tf_op jit(solution)/shard_map/all_to_all | solution.py:12
  16.8 162.2 %reduce-scatter.2.cloned.1.call-start = ((), (), s32[]{:S(2)}) async-start(), calls=%async_computation.2 | async-start | bytes 3342336 | tf_op jit(solution)/shard_map/reduce_scatter | solution.py:47
  49.0 21.7 %copy-start = (bf16[48,1024]{1,0:T(8,128)(2,1)S(1)}, bf16[48,1024]{1,0:T(8,128)(2,1)}, u32[]{:S(2)}) copy-start(bf16[48,1024]{1,0:T(8,128)(2,1)} %param.10) | copy-start | bytes 294916
  49.0 96.7 %copy-start.1 = (bf16[48,1024]{1,0:T(8,128)(2,1)S(1)}, bf16[48,1024]{1,0:T(8,128)(2,1)}, u32[]{:S(2)}) copy-start(bf16[48,1024]{1,0:T(8,128)(2,1)} %param.11) | copy-start | bytes 294916
Sparse Core Ops, SparseCore 0:
  70.8 77.7 reduce-scatter.1

commit v2 on v0

--- a/solution.py
+++ b/solution.py
@@ -13,8 +13,9 @@
     gram_two = lax.psum(
         jnp.dot(factor_mode2, factor_mode2.T, preferred_element_type=jnp.float32), "col"
     )
-    gram_three = lax.psum(
-        jnp.dot(factor_mode3, factor_mode3.T, preferred_element_type=jnp.float32), "row"
+    do_points_by_axis = lambda s0: lax.all_gather(s0, axis_name="row").sum(axis=0)
+    gram_three = do_points_by_axis(
+        jnp.dot(factor_mode3, factor_mode3.T, preferred_element_type=jnp.float32)
     )
     system = gram_two * gram_three + ridge_term * jnp.eye(rank_count, dtype=jnp.float32)
     full_two = lax.all_gather(factor_mode2, "col", axis=1, tiled=True)

time: 195 us -> 184 us (0.944)
  blocking collectives: 110 us -> 99.5 us
    psum x1 -> x0, blocking collectives: 23.6 us -> none  [body(): lax.psum(jnp.dot(factor_mode3, factor_mode3.T, preferred_element_type=jnp...]
    all_gather x0 -> x1, blocking collectives: none -> 13.1 us  [body(): lax.all_gather(s0, axis_name='row').sum(axis=0)]
where the time goes in v2:
time: 184 us
  blocking collectives  99.5 us (54%)
  matrix products  32.8 us (18%)
  waiting for transfers between devices  20.3 us (11%)
  between operations  13.5 us (7%)
  other arithmetic  11.4 us (6%)
  local copies, waits for them, and re-layouts  6.48 us (4%)
    psum x1, blocking collectives, body(): lax.psum(jnp.dot(factor_mode2, factor_mode2.T, preferred_element_type=jnp...  72.2 us
    all_gather x1, waiting for transfers between devices, body(): full_two = lax.all_gather(factor_mode2, 'col', axis=1, tiled=True)  19.6 us
    dot_general x1, matrix products, body(): jnp.einsum('trab,trb->tra', contracted, mode2_rows.astype(jnp.float32), p...  16.7 us
    all_gather x1, blocking collectives, body(): full_three = lax.all_gather(factor_mode3, 'row', axis=1, tiled=True)  14.2 us
    all_gather x1, blocking collectives, body(): lax.all_gather(s0, axis_name='row').sum(axis=0)  13.1 us
    dot_general x1, matrix products, body(): jnp.einsum('trc,tabc->trab', mode3_rows, tensor_tiles, preferred_element_...  12.1 us
    another operation x3, other arithmetic, body(): cholesky_factor = jnp.linalg.cholesky(system)  5.05 us
    another operation x2, other arithmetic, body(): lax.linalg.triangular_solve(cholesky_factor, middle, left_side=True, lowe...  4.32 us
  transfers between devices with their start and end apart: 2, of which 1 were waited for; matrix products, arithmetic and copies ran while one was open for 13% of the time, Pallas kernels for 0%

profile of v2, /device:TPU:0, one launch (start us, length us, event | category | flops | bytes accessed | tf_op | source)
XLA Modules:
  0.0 184.1 jit_solution(9080652229406300847)
XLA Ops:
  6.5 0.0 all-gather.3.cloned.1.call-start
  6.5 0.7 all-gather.3.cloned.1.call-update
  7.3 0.0 reduce-scatter.2.cloned.1.call-start
  7.3 0.7 compare_select_fusion.1
  8.0 14.2 %all_gather.14 = bf16[48,8192]{1,0:T(8,128)(2,1)S(1)} all-gather(bf16[48,1024]{1,0:T(8,128)(2,1)} %param.11), channel_id=1, replica_groups=mesh['row'=8,'col'=16] {'row'}, dimensions={1}, use_global_device_ids=true | all-gather | bytes 884736 | tf_op jit(solution)/shard_map/all_gather | solution.py:22
  22.2 0.1 copy_bitcast_fusion.2
  22.3 0.6 gather_fusion
  22.9 0.7 compare_select_fusion
  23.6 0.7 broadcast_subtract_fusion
  24.2 12.1 %fusion.6 = f32[4,48,128,128]{3,1,2,0:T(8,128)} fusion(bf16[4,128,128,128]{3,2,1,0:T(8,128)(2,1)} %param.6, bf16[4,48,128]{2,1,0:T(8,128)(2,1)S(1)} %gather_fusion), kind=kOutput, calls=%fused_computation.11 | convolution fusion | flops 805306368 | bytes 29409280 | tf_op jit(solution)/shard_map/trc,tabc->trab/dot_general | solution.py:29
  36.3 19.6 %all-gather.3.cloned.1.call-done = bf16[48,16384]{1,0:T(8,128)(2,1)} async-done(((bf16[48,1024]{1,0:T(8,128)(2,1)}), bf16[48,16384]{1,0:T(8,128)(2,1)}) %all-gather.3.cloned.1.call-update) | async-done | bytes 1572880 | tf_op jit(solution)/shard_map/all_gather | solution.py:21
  55.9 1.7 copy_bitcast_fusion.1
  57.6 0.6 gather_fusion.1
  58.1 0.0 copy-start
  58.1 0.0 copy-start.1
  58.2 16.7 %fusion = f32[4,48,1,128]{3,2,1,0:T(1,128)S(1)} fusion(f32[4,48,128,128]{3,1,2,0:T(8,128)} %fusion.6, bf16[4,48,128,1]{2,1,0,3:T(8,128)(2,1)S(1)} %bitcast.49), kind=kOutput, calls=%fused_computation.2 | convolution fusion | flops 37748736 | bytes 12730368 | tf_op jit(solution)/shard_map/trab,trb->tra/dot_general | solution.py:32
  74.9 1.5 fusion.2
  76.4 3.5 %copy.30 = f32[6,8,128,128]{3,1,2,0:T(8,128)} copy(f32[6,8,128,128]{3,2,1,0:T(8,128)S(1)} %bitcast.47) | data formatting | bytes 6291456
  79.8 0.0 reduce-scatter.2.cloned.1.call-update
  79.9 0.0 copy-done
  79.9 0.1 fusion.18
  80.0 13.1 %all-gather = f32[384,48]{1,0:T(8,128)S(1)} all-gather(f32[48,48]{1,0:T(8,128)S(1)} %fusion.18), channel_id=2, replica_groups=mesh['row'=8,'col'=16] {'row'}, dimensions={0}, use_global_device_ids=true | all-gather | bytes 82944 | tf_op jit(solution)/shard_map/all_gather | solution.py:16
  93.2 0.0 copy-done.1
  93.2 0.1 fusion.17
  93.3 72.2 %psum.7 = f32[48,48]{1,0:T(8,128)S(1)} all-reduce(f32[48,48]{1,0:T(8,128)S(1)} %fusion.17), channel_id=1, replica_groups=mesh['row'=8,'col'=16] {'col'}, use_global_device_ids=true, to_apply=%region_0.0 | all-reduce | flops 2304 | bytes 18432 | tf_op jit(solution)/shard_map/psum | solution.py:13
  165.5 0.1 copy.9
  165.6 4.4 %cholesky.16 = f32[48,48]{1,0:T(8,128)S(1)} custom-call(f32[48,48]{1,0:T(8,128)S(1)} %fusion.13), custom_call_target="Cholesky" | custom-call | tf_op jit(solution)/shard_map/jit(cholesky)/cholesky | solution.py:44
  170.0 0.6 compare_reduce_fusion
  170.7 0.7 fusion.8
  171.3 3.7 %custom-call.8 = f32[1,48,48]{1,2,0:T(8,128)S(1)} custom-call(f32[1,48,48]{2,1,0:T(8,128)S(1)} %fusion.8), custom_call_target="InvertDiagBlocksLowerTriangular" | custom-call | tf_op jit(solution)/shard_map/triangular_solve | solution.py:46
  175.0 0.0 reduce-scatter.2.cloned.1.call-done
  175.0 1.3 fusion.11
  176.3 1.0 fusion.9
  (6 shorter events, 0.1 us)
Async XLA Ops:
  6.5 49.4 %all-gather.3.cloned.1.call-start = ((), (), s32[]{:S(2)}) async-start(), calls=%async_computation.1 | async-start | bytes 1671168 | tf_op jit(solution)/shard_map/all_gather | solution.py:21
  7.3 167.8 %reduce-scatter.2.cloned.1.call-start = ((), (), s32[]{:S(2)}) async-start(), calls=%async_computation.2 | async-start | bytes 3342336 | tf_op jit(solution)/shard_map/reduce_scatter | solution.py:43
  58.1 21.7 %copy-start = (bf16[48,1024]{1,0:T(8,128)(2,1)S(1)}, bf16[48,1024]{1,0:T(8,128)(2,1)}, u32[]{:S(2)}) copy-start(bf16[48,1024]{1,0:T(8,128)(2,1)} %param.11) | copy-start | bytes 294916
  58.1 35.0 %copy-start.1 = (bf16[48,1024]{1,0:T(8,128)(2,1)S(1)}, bf16[48,1024]{1,0:T(8,128)(2,1)}, u32[]{:S(2)}) copy-start(bf16[48,1024]{1,0:T(8,128)(2,1)} %param.10) | copy-start | bytes 294916
Sparse Core Ops, SparseCore 0:
  9.5 46.3 all-gather.2
  80.0 75.9 reduce-scatter.1
